TPU v7x, 512 devices: a whole 4x8x8 slice. The times are simulated.
512 devices in a mesh: gy: 32 (over z, x), gx: 16 (over y, core).
Axes of the slice: x: 4, y: 8, z: 8, core: 2. Of those that a mesh axis runs over, the one named last changes fastest.
Arguments:
- ensemble: float32 [64, 256, 2048], P(None, 'gy', 'gx'), may hold values from -6 to 6
- flow: float32 [3, 256, 2048], P(None, 'gy', 'gx')
- obs_cell: int32 [32, 16, 4], P('gy', 'gx'), may hold values from 0 to 1023
- obs_value: float32 [32, 16, 4], P('gy', 'gx'), may hold values from -6 to 6
- obs_var: float32 [32, 16, 4], P('gy', 'gx'), may hold values from 4 to 16
Outputs:
- analysis: float32 [64, 256, 2048], P(None, 'gy', 'gx')
All inputs are finite; a program needn't handle non-finite values.
Results may differ from a plain program's by a relative error of at most 0.0001.
Values sent between devices are 32-bit elements; how exact they have to be, the bound alone decides.
A program may use at most 64 MiB of HBM per device.

v0:
```python
import jax
import jax.numpy as jnp
from jax import lax
from jax.sharding import PartitionSpec as P


def extended(block, sides, width):
    for axis, dim in sides:
        count = lax.axis_size(axis)
        forward = [(i, i + 1) for i in range(count - 1)]
        backward = [(target, source) for source, target in forward]
        low = lax.ppermute(
            lax.slice_in_dim(block, block.shape[dim] - width, None, axis=dim), axis, forward
        )
        high = lax.ppermute(lax.slice_in_dim(block, 0, width, axis=dim), axis, backward)
        block = jnp.concatenate([low, block, high], axis=dim)
    return block


def advance(padded, coeffs):
    state_grid = padded[:, 1:-1, 1:-1]
    north = padded[:, :-2, 1:-1]
    south = padded[:, 2:, 1:-1]
    west = padded[:, 1:-1, :-2]
    east = padded[:, 1:-1, 2:]
    spread = coeffs[0] * (north + south + west + east - 4.0 * state_grid)
    return state_grid + spread - 0.5 * coeffs[1] * (east - west) - 0.5 * coeffs[2] * (south - north)


def border_update(state_grid, flow):
    padded = extended(state_grid, (("gy", 1), ("gx", 2)), 1)
    return advance(padded, flow)


def tri_solve(matrix, rhs):
    return lax.linalg.triangular_solve(matrix, rhs, left_side=True, lower=True, transpose_a=True)


def body(ensemble, flow, obs_cell, obs_value, obs_var):
    members = ensemble.shape[0]
    predicted_state = border_update(border_update(ensemble, flow), flow)
    ensemble_average = jnp.mean(predicted_state, axis=0)
    member_deviation = predicted_state - ensemble_average
    flat_anomaly = member_deviation.reshape(members, -1)
    cells = obs_cell.reshape(-1)
    factor = lax.rsqrt(obs_var.reshape(-1))
    scaled = jnp.take(flat_anomaly, cells, axis=1) * factor
    innovation = (obs_value.reshape(-1) - jnp.take(ensemble_average.reshape(-1), cells)) * factor
    eye = jnp.eye(members, dtype=jnp.float32)
    local_gram = jnp.dot(scaled, scaled.T, precision=lax.Precision.HIGHEST)
    local_target = jnp.dot(scaled, innovation, precision=lax.Precision.HIGHEST)
    gram, target = lax.psum((local_gram, local_target), ("gy", "gx"))
    lower = jnp.linalg.cholesky(gram + (members - 1.0) * eye)
    inverse = tri_solve(lower, eye)
    weights = jnp.dot(
        inverse,
        jnp.dot(inverse.T, target, precision=lax.Precision.HIGHEST),
        precision=lax.Precision.HIGHEST,
    )
    transform = jnp.sqrt(members - 1.0) * inverse + weights[:, None]
    update = jnp.dot(transform.T, flat_anomaly, precision=lax.Precision.HIGHEST)
    return ensemble_average + update.reshape(member_deviation.shape)


def solution(mesh):
    return jax.shard_map(
        body,
        mesh=mesh,
        in_specs=(
            P(None, "gy", "gx"),
            P(None, "gy", "gx"),
            P("gy", "gx", None),
            P("gy", "gx", None),
            P("gy", "gx", None),
        ),
        out_specs=P(None, "gy", "gx"),
        check_vma=False,
    )
```

profile of v0, /device:TPU:1, one launch (start us, length us, event | category | flops | bytes accessed | tf_op | source)
XLA Modules:
  0.0 169.7 jit_solution(2727058517683121358)
XLA Ops:
  0.0 0.0 copy-start
  0.0 1.1 copy.23
  1.1 0.0 copy-start.1
  1.1 3.9 %collective-permute-start = (f32[64,1,128]{2,0,1:T(8,128)S(1)}, f32[64,1,128]{2,0,1:T(8,128)S(1)}, u32[]{:S(2)}, u32[]{:S(2)}) collective-permute-start(f32[64,1,128]{2,0,1:T(8,128)S(1)} %get-tuple-element.18), channel_id=1, source_target_pairs={{0,16},{16,32},{32,48},{48,64},{64,80},{80,96},{96,112},{112,128},... | collective-permute-start | bytes 98312 | tf_op jit(solution)/shard_map/ppermute | solution.py:12
  5.1 0.0 copy-start.2
  5.1 1.3 collective-permute-start.1
  6.4 0.0 copy-done.1
  6.4 0.0 copy-done.2
  6.4 0.0 collective-permute-done
  6.4 0.0 copy-done
  6.5 3.2 %collective-permute-done.1 = f32[64,1,128]{2,0,1:T(8,128)S(1)} collective-permute-done((f32[64,1,128]{2,0,1:T(8,128)S(1)}, f32[64,1,128]{2,0,1:T(8,128)S(1)}, u32[]{:S(2)}, u32[]{:S(2)}) %collective-permute-start.1) | collective-permute-done | bytes 32800 | tf_op jit(solution)/shard_map/ppermute | solution.py:15
  9.7 0.2 fusion.34
  9.9 5.2 %collective-permute-start.2 = (f32[64,10,1]{2,0,1:T(8,128)S(1)}, f32[64,10,1]{2,0,1:T(8,128)S(1)}, u32[]{:S(2)}, u32[]{:S(2)}) collective-permute-start(f32[64,10,1]{2,0,1:T(8,128)S(1)} %get-tuple-element.11), channel_id=1, source_target_pairs={{0,1},{1,2},{2,3},{3,4},{4,5},{5,6},{6,7},{7,8},{8,9},{9,10},{10,1... | collective-permute-start | bytes 7688 | tf_op jit(solution)/shard_map/ppermute | solution.py:12
  15.1 3.4 %collective-permute-start.3 = (f32[64,10,1]{2,0,1:T(8,128)S(1)}, f32[64,10,1]{2,0,1:T(8,128)S(1)}, u32[]{:S(2)}, u32[]{:S(2)}) collective-permute-start(f32[64,10,1]{2,0,1:T(8,128)S(1)} %get-tuple-element.12), channel_id=1, source_target_pairs={{1,0},{2,1},{3,2},{4,3},{5,4},{6,5},{7,6},{8,7},{9,8},{10,9},{11,1... | collective-permute-start | bytes 7688 | tf_op jit(solution)/shard_map/ppermute | solution.py:15
  18.5 0.6 collective-permute-done.2
  19.1 4.4 %collective-permute-done.3 = f32[64,10,1]{2,0,1:T(8,128)S(1)} collective-permute-done((f32[64,10,1]{2,0,1:T(8,128)S(1)}, f32[64,10,1]{2,0,1:T(8,128)S(1)}, u32[]{:S(2)}, u32[]{:S(2)}) %collective-permute-start.3) | collective-permute-done | bytes 2592 | tf_op jit(solution)/shard_map/ppermute | solution.py:15
  23.5 0.3 multiply_subtract_fusion.1
  23.8 0.0 copy-start.3
  23.8 3.1 %collective-permute-start.4 = (f32[64,1,128]{2,0,1:T(8,128)S(1)}, f32[64,1,128]{2,0,1:T(8,128)S(1)}, u32[]{:S(2)}, u32[]{:S(2)}) collective-permute-start(f32[64,1,128]{2,0,1:T(8,128)S(1)} %get-tuple-element.15), channel_id=1, source_target_pairs={{0,16},{16,32},{32,48},{48,64},{64,80},{80,96},{96,112},{112,128},... | collective-permute-start | bytes 98312 | tf_op jit(solution)/shard_map/ppermute | solution.py:12
  26.9 1.3 collective-permute-start.5
  28.2 0.0 copy-done.3
  28.3 0.0 collective-permute-done.4
  28.3 3.3 %collective-permute-done.5 = f32[64,1,128]{2,0,1:T(8,128)S(1)} collective-permute-done((f32[64,1,128]{2,0,1:T(8,128)S(1)}, f32[64,1,128]{2,0,1:T(8,128)S(1)}, u32[]{:S(2)}, u32[]{:S(2)}) %collective-permute-start.5) | collective-permute-done | bytes 32800 | tf_op jit(solution)/shard_map/ppermute | solution.py:15
  31.6 0.2 fusion.33
  31.8 3.2 %collective-permute-start.6 = (f32[64,10,1]{2,0,1:T(8,128)S(1)}, f32[64,10,1]{2,0,1:T(8,128)S(1)}, u32[]{:S(2)}, u32[]{:S(2)}) collective-permute-start(f32[64,10,1]{2,0,1:T(8,128)S(1)} %get-tuple-element.9), channel_id=1, source_target_pairs={{0,1},{1,2},{2,3},{3,4},{4,5},{5,6},{6,7},{7,8},{8,9},{9,10},{10,1... | collective-permute-start | bytes 7688 | tf_op jit(solution)/shard_map/ppermute | solution.py:12
  35.0 1.9 %collective-permute-start.7 = (f32[64,10,1]{2,0,1:T(8,128)S(1)}, f32[64,10,1]{2,0,1:T(8,128)S(1)}, u32[]{:S(2)}, u32[]{:S(2)}) collective-permute-start(f32[64,10,1]{2,0,1:T(8,128)S(1)} %get-tuple-element.10), channel_id=1, source_target_pairs={{1,0},{2,1},{3,2},{4,3},{5,4},{6,5},{7,6},{8,7},{9,8},{10,9},{11,1... | collective-permute-start | bytes 7688 | tf_op jit(solution)/shard_map/ppermute | solution.py:15
  36.9 2.1 %collective-permute-done.6 = f32[64,10,1]{2,0,1:T(8,128)S(1)} collective-permute-done((f32[64,10,1]{2,0,1:T(8,128)S(1)}, f32[64,10,1]{2,0,1:T(8,128)S(1)}, u32[]{:S(2)}, u32[]{:S(2)}) %collective-permute-start.6) | collective-permute-done | bytes 2592 | tf_op jit(solution)/shard_map/ppermute | solution.py:12
  39.0 4.4 %collective-permute-done.7 = f32[64,10,1]{2,0,1:T(8,128)S(1)} collective-permute-done((f32[64,10,1]{2,0,1:T(8,128)S(1)}, f32[64,10,1]{2,0,1:T(8,128)S(1)}, u32[]{:S(2)}, u32[]{:S(2)}) %collective-permute-start.7) | collective-permute-done | bytes 2592 | tf_op jit(solution)/shard_map/ppermute | solution.py:15
  43.4 0.3 fusion.32
  43.7 0.2 copy.25
  43.9 0.6 gather_fusion
  44.5 0.6 gather_fusion.1
  45.1 0.0 copy-start.4
  45.1 0.3 fusion.13
  45.4 0.3 copy-done.4
  45.8 0.2 convolution_bitcast_fusion.2
  46.0 109.7 %all-reduce = (f32[64,64]{1,0:T(8,128)S(1)}, f32[64]{0:T(128)S(1)}) all-reduce(f32[64,64]{1,0:T(8,128)S(1)} %fusion.13, f32[64]{0:T(128)S(1)} %convolution_bitcast_fusion.2), channel_id=1, replica_groups=mesh['gy'=32,'gx'=16] {'gy','gx'}, use_global_device_ids=true, to_apply=%region_1.2 | all-reduce | flops 4160 | bytes 33280 | tf_op jit(solution)/shard_map/psum | solution.py:52
  155.7 0.1 copy.26
  155.8 5.8 %cholesky.17 = f32[64,64]{1,0:T(8,128)S(1)} custom-call(f32[64,64]{1,0:T(8,128)S(1)} %fusion.7), custom_call_target="Cholesky" | custom-call | tf_op jit(solution)/shard_map/jit(cholesky)/cholesky | solution.py:53
  161.6 0.6 compare_reduce_fusion
  162.3 0.7 fusion.2
  162.9 4.9 %custom-call.6 = f32[1,64,64]{1,2,0:T(8,128)S(1)} custom-call(f32[1,64,64]{2,1,0:T(8,128)S(1)} %fusion.2), custom_call_target="InvertDiagBlocksLowerTriangular" | custom-call | tf_op jit(solution)/shard_map/triangular_solve | solution.py:36
  167.8 0.2 fusion.5
  168.0 0.1 convolution_bitcast_fusion.1
  168.2 0.2 convolution_bitcast_fusion
  168.3 0.5 convolution_add_fusion
  168.8 0.9 copy.29
  (16 shorter events, 0.2 us)
Async XLA Ops:
  0.0 6.4 %copy-start = (f32[64,8,128]{2,1,0:T(8,128)S(1)}, f32[64,8,128]{2,1,0:T(8,128)}, u32[]{:S(2)}) copy-start(f32[64,8,128]{2,1,0:T(8,128)} %param.5) | copy-start | bytes 786436
  1.1 5.3 %copy-start.1 = (f32[3,8,128]{2,1,0:T(8,128)S(1)}, f32[3,8,128]{2,1,0:T(8,128)}, u32[]{:S(2)}) copy-start(f32[3,8,128]{2,1,0:T(8,128)} %param.6) | copy-start | bytes 36868
  1.1 5.3 %collective-permute-start = (f32[64,1,128]{2,0,1:T(8,128)S(1)}, f32[64,1,128]{2,0,1:T(8,128)S(1)}, u32[]{:S(2)}, u32[]{:S(2)}) collective-permute-start(f32[64,1,128]{2,0,1:T(8,128)S(1)} %get-tuple-element.18), channel_id=1, source_target_pairs={{0,16},{16,32},{32,48},{48,64},{64,80},{80,96},{96,112},{112,128},... | collective-permute-start | bytes 98312 | tf_op jit(solution)/shard_map/ppermute | solution.py:12
  5.1 1.3 copy-start.2
  5.1 4.7 %collective-permute-start.1 = (f32[64,1,128]{2,0,1:T(8,128)S(1)}, f32[64,1,128]{2,0,1:T(8,128)S(1)}, u32[]{:S(2)}, u32[]{:S(2)}) collective-permute-start(f32[64,1,128]{2,0,1:T(8,128)S(1)} %get-tuple-element.17), channel_id=1, source_target_pairs={{16,0},{32,16},{48,32},{64,48},{80,64},{96,80},{112,96},{128,112},... | collective-permute-start | bytes 98312 | tf_op jit(solution)/shard_map/ppermute | solution.py:15
  9.9 9.2 %collective-permute-start.2 = (f32[64,10,1]{2,0,1:T(8,128)S(1)}, f32[64,10,1]{2,0,1:T(8,128)S(1)}, u32[]{:S(2)}, u32[]{:S(2)}) collective-permute-start(f32[64,10,1]{2,0,1:T(8,128)S(1)} %get-tuple-element.11), channel_id=1, source_target_pairs={{0,1},{1,2},{2,3},{3,4},{4,5},{5,6},{6,7},{7,8},{8,9},{9,10},{10,1... | collective-permute-start | bytes 7688 | tf_op jit(solution)/shard_map/ppermute | solution.py:12
  15.1 8.4 %collective-permute-start.3 = (f32[64,10,1]{2,0,1:T(8,128)S(1)}, f32[64,10,1]{2,0,1:T(8,128)S(1)}, u32[]{:S(2)}, u32[]{:S(2)}) collective-permute-start(f32[64,10,1]{2,0,1:T(8,128)S(1)} %get-tuple-element.12), channel_id=1, source_target_pairs={{1,0},{2,1},{3,2},{4,3},{5,4},{6,5},{7,6},{8,7},{9,8},{10,9},{11,1... | collective-permute-start | bytes 7688 | tf_op jit(solution)/shard_map/ppermute | solution.py:15
  23.8 4.4 %copy-start.3 = (f32[1,1,4]{2,1,0:T(1,128)S(1)}, f32[1,1,4]{2,1,0:T(1,128)}, u32[]{:S(2)}) copy-start(f32[1,1,4]{2,1,0:T(1,128)} %param.9) | copy-start | bytes 52
  23.8 4.5 %collective-permute-start.4 = (f32[64,1,128]{2,0,1:T(8,128)S(1)}, f32[64,1,128]{2,0,1:T(8,128)S(1)}, u32[]{:S(2)}, u32[]{:S(2)}) collective-permute-start(f32[64,1,128]{2,0,1:T(8,128)S(1)} %get-tuple-element.15), channel_id=1, source_target_pairs={{0,16},{16,32},{32,48},{48,64},{64,80},{80,96},{96,112},{112,128},... | collective-permute-start | bytes 98312 | tf_op jit(solution)/shard_map/ppermute | solution.py:12
  26.9 4.7 %collective-permute-start.5 = (f32[64,1,128]{2,0,1:T(8,128)S(1)}, f32[64,1,128]{2,0,1:T(8,128)S(1)}, u32[]{:S(2)}, u32[]{:S(2)}) collective-permute-start(f32[64,1,128]{2,0,1:T(8,128)S(1)} %get-tuple-element.16), channel_id=1, source_target_pairs={{16,0},{32,16},{48,32},{64,48},{80,64},{96,80},{112,96},{128,112},... | collective-permute-start | bytes 98312 | tf_op jit(solution)/shard_map/ppermute | solution.py:15
  31.8 7.2 %collective-permute-start.6 = (f32[64,10,1]{2,0,1:T(8,128)S(1)}, f32[64,10,1]{2,0,1:T(8,128)S(1)}, u32[]{:S(2)}, u32[]{:S(2)}) collective-permute-start(f32[64,10,1]{2,0,1:T(8,128)S(1)} %get-tuple-element.9), channel_id=1, source_target_pairs={{0,1},{1,2},{2,3},{3,4},{4,5},{5,6},{6,7},{7,8},{8,9},{9,10},{10,1... | collective-permute-start | bytes 7688 | tf_op jit(solution)/shard_map/ppermute | solution.py:12
  35.0 8.4 %collective-permute-start.7 = (f32[64,10,1]{2,0,1:T(8,128)S(1)}, f32[64,10,1]{2,0,1:T(8,128)S(1)}, u32[]{:S(2)}, u32[]{:S(2)}) collective-permute-start(f32[64,10,1]{2,0,1:T(8,128)S(1)} %get-tuple-element.10), channel_id=1, source_target_pairs={{1,0},{2,1},{3,2},{4,3},{5,4},{6,5},{7,6},{8,7},{9,8},{10,9},{11,1... | collective-permute-start | bytes 7688 | tf_op jit(solution)/shard_map/ppermute | solution.py:15
  45.1 0.7 copy-start.4
where the time goes:
time: 170 us
  blocking collectives  110 us (65%)
  starting transfers between devices  23.3 us (14%)
  waiting for transfers between devices  18 us (11%)
  other arithmetic  12.8 us (8%)
  local copies, waits for them, and re-layouts  4.15 us (2%)
    psum x1, blocking collectives, body(): gram, target = lax.psum((local_gram, local_target), ('gy', 'gx'))  110 us
    ppermute x4, starting transfers between devices, extended(): lax.ppermute(lax.slice_in_dim(block, block.shape[dim] - width, None, axis...  15.4 us
    ppermute x4, waiting for transfers between devices, extended(): lax.ppermute(lax.slice_in_dim(block, 0, width, axis=dim), axis, backward)  15.3 us
    ppermute x4, starting transfers between devices, extended(): lax.ppermute(lax.slice_in_dim(block, 0, width, axis=dim), axis, backward)  7.9 us
    another operation x3, other arithmetic, body(): lower = jnp.linalg.cholesky(gram + (members - 1.0) * eye)  6.52 us
    another operation x2, other arithmetic, tri_solve(): lax.linalg.triangular_solve(matrix, rhs, left_side=True, lower=True, tran...  5.55 us
  transfers between devices with their start and end apart: 8, of which 6 were waited for; matrix products, arithmetic and copies ran while one was open for 0% of the time, Pallas kernels for 0%

commit v1 on v0

--- a/solution.py
+++ b/solution.py
@@ -49,7 +49,7 @@
     eye = jnp.eye(members, dtype=jnp.float32)
     local_gram = jnp.dot(scaled, scaled.T, precision=lax.Precision.HIGHEST)
     local_target = jnp.dot(scaled, innovation, precision=lax.Precision.HIGHEST)
-    gram, target = lax.psum((local_gram, local_target), ("gy", "gx"))
+    gram, target = lax.psum(lax.psum((local_gram, local_target), "gx"), "gy")
     lower = jnp.linalg.cholesky(gram + (members - 1.0) * eye)
     inverse = tri_solve(lower, eye)
     weights = jnp.dot(

time: 170 us -> 255 us (1.50)
  the two profiles are of different devices: /device:TPU:1 before, /device:TPU:288 now
where the time goes in v1:
time: 255 us
  blocking collectives  192 us (75%)
  starting transfers between devices  32.2 us (13%)
  other arithmetic  12.8 us (5%)
  waiting for transfers between devices  12.1 us (5%)
  local copies, waits for them, and re-layouts  4.15 us (2%)
    psum x2, blocking collectives, body(): gram, target = lax.psum(lax.psum((local_gram, local_target), 'gx'), 'gy')  192 us
    ppermute x4, starting transfers between devices, extended(): lax.ppermute(lax.slice_in_dim(block, 0, width, axis=dim), axis, backward)  23 us
    ppermute x4, starting transfers between devices, extended(): lax.ppermute(lax.slice_in_dim(block, block.shape[dim] - width, None, axis...  9.16 us
    another operation x3, other arithmetic, body(): lower = jnp.linalg.cholesky(gram + (members - 1.0) * eye)  6.52 us
    ppermute x4, waiting for transfers between devices, extended(): lax.ppermute(lax.slice_in_dim(block, 0, width, axis=dim), axis, backward)  6.5 us
    ppermute x4, waiting for transfers between devices, extended(): lax.ppermute(lax.slice_in_dim(block, block.shape[dim] - width, None, axis...  5.61 us
    another operation x2, other arithmetic, tri_solve(): lax.linalg.triangular_solve(matrix, rhs, left_side=True, lower=True, tran...  5.55 us
  transfers between devices with their start and end apart: 8, of which 6 were waited for; matrix products, arithmetic and copies ran while one was open for 0% of the time, Pallas kernels for 0%

profile of v1, /device:TPU:288, one launch (start us, length us, event | category | flops | bytes accessed | tf_op | source)
XLA Modules:
  0.0 255.1 jit_solution(14150878703178750606)
XLA Ops:
  0.0 0.0 copy-start
  0.0 1.1 copy.23
  1.1 0.0 copy-start.1
  1.1 3.4 %collective-permute-start = (f32[64,1,128]{2,0,1:T(8,128)S(1)}, f32[64,1,128]{2,0,1:T(8,128)S(1)}, u32[]{:S(2)}, u32[]{:S(2)}) collective-permute-start(f32[64,1,128]{2,0,1:T(8,128)S(1)} %get-tuple-element.20), channel_id=1, source_target_pairs={{0,16},{16,32},{32,48},{48,64},{64,80},{80,96},{96,112},{112,128},... | collective-permute-start | bytes 98312 | tf_op jit(solution)/shard_map/ppermute | solution.py:12
  4.5 0.0 copy-start.2
  4.5 5.8 %collective-permute-start.1 = (f32[64,1,128]{2,0,1:T(8,128)S(1)}, f32[64,1,128]{2,0,1:T(8,128)S(1)}, u32[]{:S(2)}, u32[]{:S(2)}) collective-permute-start(f32[64,1,128]{2,0,1:T(8,128)S(1)} %get-tuple-element.19), channel_id=1, source_target_pairs={{16,0},{32,16},{48,32},{64,48},{80,64},{96,80},{112,96},{128,112},... | collective-permute-start | bytes 98312 | tf_op jit(solution)/shard_map/ppermute | solution.py:15
  10.3 0.0 copy-done.1
  10.3 0.0 copy-done.2
  10.3 0.0 collective-permute-done
  10.4 0.0 copy-done
  10.4 1.4 collective-permute-done.1
  11.9 0.2 fusion.34
  12.0 1.9 collective-permute-start.2
  14.0 4.9 %collective-permute-start.3 = (f32[64,10,1]{2,0,1:T(8,128)S(1)}, f32[64,10,1]{2,0,1:T(8,128)S(1)}, u32[]{:S(2)}, u32[]{:S(2)}) collective-permute-start(f32[64,10,1]{2,0,1:T(8,128)S(1)} %get-tuple-element.14), channel_id=1, source_target_pairs={{1,0},{2,1},{3,2},{4,3},{5,4},{6,5},{7,6},{8,7},{9,8},{10,9},{11,1... | collective-permute-start | bytes 7688 | tf_op jit(solution)/shard_map/ppermute | solution.py:15
  18.8 2.8 %collective-permute-done.2 = f32[64,10,1]{2,0,1:T(8,128)S(1)} collective-permute-done((f32[64,10,1]{2,0,1:T(8,128)S(1)}, f32[64,10,1]{2,0,1:T(8,128)S(1)}, u32[]{:S(2)}, u32[]{:S(2)}) %collective-permute-start.2) | collective-permute-done | bytes 2592 | tf_op jit(solution)/shard_map/ppermute | solution.py:12
  21.6 1.8 collective-permute-done.3
  23.4 0.3 multiply_subtract_fusion.1
  23.7 0.0 copy-start.3
  23.7 1.9 collective-permute-start.4
  25.6 7.5 %collective-permute-start.5 = (f32[64,1,128]{2,0,1:T(8,128)S(1)}, f32[64,1,128]{2,0,1:T(8,128)S(1)}, u32[]{:S(2)}, u32[]{:S(2)}) collective-permute-start(f32[64,1,128]{2,0,1:T(8,128)S(1)} %get-tuple-element.18), channel_id=1, source_target_pairs={{16,0},{32,16},{48,32},{64,48},{80,64},{96,80},{112,96},{128,112},... | collective-permute-start | bytes 98312 | tf_op jit(solution)/shard_map/ppermute | solution.py:15
  33.2 0.0 copy-done.3
  33.2 0.0 collective-permute-done.4
  33.2 1.5 collective-permute-done.5
  34.8 0.2 fusion.33
  35.0 1.9 collective-permute-start.6
  36.9 4.9 %collective-permute-start.7 = (f32[64,10,1]{2,0,1:T(8,128)S(1)}, f32[64,10,1]{2,0,1:T(8,128)S(1)}, u32[]{:S(2)}, u32[]{:S(2)}) collective-permute-start(f32[64,10,1]{2,0,1:T(8,128)S(1)} %get-tuple-element.12), channel_id=1, source_target_pairs={{1,0},{2,1},{3,2},{4,3},{5,4},{6,5},{7,6},{8,7},{9,8},{10,9},{11,1... | collective-permute-start | bytes 7688 | tf_op jit(solution)/shard_map/ppermute | solution.py:15
  41.8 2.8 %collective-permute-done.6 = f32[64,10,1]{2,0,1:T(8,128)S(1)} collective-permute-done((f32[64,10,1]{2,0,1:T(8,128)S(1)}, f32[64,10,1]{2,0,1:T(8,128)S(1)}, u32[]{:S(2)}, u32[]{:S(2)}) %collective-permute-start.6) | collective-permute-done | bytes 2592 | tf_op jit(solution)/shard_map/ppermute | solution.py:12
  44.6 1.8 collective-permute-done.7
  46.3 0.3 fusion.32
  46.7 0.2 copy.25
  46.9 0.6 gather_fusion
  47.4 0.6 gather_fusion.1
  48.1 0.0 copy-start.4
  48.1 0.3 fusion.13
  48.4 0.3 copy-done.4
  48.7 0.2 convolution_bitcast_fusion.2
  48.9 48.8 %all-reduce.1 = (f32[64,64]{1,0:T(8,128)S(1)}, f32[64]{0:T(128)S(1)}) all-reduce(f32[64,64]{1,0:T(8,128)S(1)} %fusion.13, f32[64]{0:T(128)S(1)} %convolution_bitcast_fusion.2), channel_id=1, replica_groups=mesh['gy'=32,'gx'=16] {'gx'}, use_global_device_ids=true, to_apply=%region_1.2 | all-reduce | flops 4160 | bytes 33280 | tf_op jit(solution)/shard_map/psum | solution.py:52
  97.7 143.3 %all-reduce = (f32[64,64]{1,0:T(8,128)S(1)}, f32[64]{0:T(128)S(1)}) all-reduce(f32[64,64]{1,0:T(8,128)S(1)} %get-tuple-element.7, f32[64]{0:T(128)S(1)} %get-tuple-element.8), channel_id=1, replica_groups=mesh['gy'=32,'gx'=16] {'gy'}, use_global_device_ids=true, to_apply=%region_2.3 | all-reduce | flops 4160 | bytes 33280 | tf_op jit(solution)/shard_map/psum | solution.py:52
  241.0 0.1 copy.26
  241.1 5.8 %cholesky.17 = f32[64,64]{1,0:T(8,128)S(1)} custom-call(f32[64,64]{1,0:T(8,128)S(1)} %fusion.7), custom_call_target="Cholesky" | custom-call | tf_op jit(solution)/shard_map/jit(cholesky)/cholesky | solution.py:53
  247.0 0.6 compare_reduce_fusion
  247.7 0.7 fusion.2
  248.3 4.9 %custom-call.6 = f32[1,64,64]{1,2,0:T(8,128)S(1)} custom-call(f32[1,64,64]{2,1,0:T(8,128)S(1)} %fusion.2), custom_call_target="InvertDiagBlocksLowerTriangular" | custom-call | tf_op jit(solution)/shard_map/triangular_solve | solution.py:36
  253.2 0.2 fusion.5
  253.4 0.1 convolution_bitcast_fusion.1
  253.5 0.2 convolution_bitcast_fusion
  253.7 0.5 convolution_add_fusion
  254.2 0.9 copy.29
  (16 shorter events, 0.2 us)
Async XLA Ops:
  0.0 10.4 %copy-start = (f32[64,8,128]{2,1,0:T(8,128)S(1)}, f32[64,8,128]{2,1,0:T(8,128)}, u32[]{:S(2)}) copy-start(f32[64,8,128]{2,1,0:T(8,128)} %param.5) | copy-start | bytes 786436
  1.1 9.2 %copy-start.1 = (f32[3,8,128]{2,1,0:T(8,128)S(1)}, f32[3,8,128]{2,1,0:T(8,128)}, u32[]{:S(2)}) copy-start(f32[3,8,128]{2,1,0:T(8,128)} %param.6) | copy-start | bytes 36868
  1.1 9.2 %collective-permute-start = (f32[64,1,128]{2,0,1:T(8,128)S(1)}, f32[64,1,128]{2,0,1:T(8,128)S(1)}, u32[]{:S(2)}, u32[]{:S(2)}) collective-permute-start(f32[64,1,128]{2,0,1:T(8,128)S(1)} %get-tuple-element.20), channel_id=1, source_target_pairs={{0,16},{16,32},{32,48},{48,64},{64,80},{80,96},{96,112},{112,128},... | collective-permute-start | bytes 98312 | tf_op jit(solution)/shard_map/ppermute | solution.py:12
  4.5 5.8 %copy-start.2 = (s32[1,1,4]{2,1,0:T(1,128)S(1)}, s32[1,1,4]{2,1,0:T(1,128)}, u32[]{:S(2)}) copy-start(s32[1,1,4]{2,1,0:T(1,128)} %param.7) | copy-start | bytes 52
  4.5 7.3 %collective-permute-start.1 = (f32[64,1,128]{2,0,1:T(8,128)S(1)}, f32[64,1,128]{2,0,1:T(8,128)S(1)}, u32[]{:S(2)}, u32[]{:S(2)}) collective-permute-start(f32[64,1,128]{2,0,1:T(8,128)S(1)} %get-tuple-element.19), channel_id=1, source_target_pairs={{16,0},{32,16},{48,32},{64,48},{80,64},{96,80},{112,96},{128,112},... | collective-permute-start | bytes 98312 | tf_op jit(solution)/shard_map/ppermute | solution.py:15
  12.0 9.6 %collective-permute-start.2 = (f32[64,10,1]{2,0,1:T(8,128)S(1)}, f32[64,10,1]{2,0,1:T(8,128)S(1)}, u32[]{:S(2)}, u32[]{:S(2)}) collective-permute-start(f32[64,10,1]{2,0,1:T(8,128)S(1)} %get-tuple-element.13), channel_id=1, source_target_pairs={{0,1},{1,2},{2,3},{3,4},{4,5},{5,6},{6,7},{7,8},{8,9},{9,10},{10,1... | collective-permute-start | bytes 7688 | tf_op jit(solution)/shard_map/ppermute | solution.py:12
  14.0 9.4 %collective-permute-start.3 = (f32[64,10,1]{2,0,1:T(8,128)S(1)}, f32[64,10,1]{2,0,1:T(8,128)S(1)}, u32[]{:S(2)}, u32[]{:S(2)}) collective-permute-start(f32[64,10,1]{2,0,1:T(8,128)S(1)} %get-tuple-element.14), channel_id=1, source_target_pairs={{1,0},{2,1},{3,2},{4,3},{5,4},{6,5},{7,6},{8,7},{9,8},{10,9},{11,1... | collective-permute-start | bytes 7688 | tf_op jit(solution)/shard_map/ppermute | solution.py:15
  23.7 9.5 %copy-start.3 = (f32[1,1,4]{2,1,0:T(1,128)S(1)}, f32[1,1,4]{2,1,0:T(1,128)}, u32[]{:S(2)}) copy-start(f32[1,1,4]{2,1,0:T(1,128)} %param.9) | copy-start | bytes 52
  23.7 9.5 %collective-permute-start.4 = (f32[64,1,128]{2,0,1:T(8,128)S(1)}, f32[64,1,128]{2,0,1:T(8,128)S(1)}, u32[]{:S(2)}, u32[]{:S(2)}) collective-permute-start(f32[64,1,128]{2,0,1:T(8,128)S(1)} %get-tuple-element.17), channel_id=1, source_target_pairs={{0,16},{16,32},{32,48},{48,64},{64,80},{80,96},{96,112},{112,128},... | collective-permute-start | bytes 98312 | tf_op jit(solution)/shard_map/ppermute | solution.py:12
  25.6 9.1 %collective-permute-start.5 = (f32[64,1,128]{2,0,1:T(8,128)S(1)}, f32[64,1,128]{2,0,1:T(8,128)S(1)}, u32[]{:S(2)}, u32[]{:S(2)}) collective-permute-start(f32[64,1,128]{2,0,1:T(8,128)S(1)} %get-tuple-element.18), channel_id=1, source_target_pairs={{16,0},{32,16},{48,32},{64,48},{80,64},{96,80},{112,96},{128,112},... | collective-permute-start | bytes 98312 | tf_op jit(solution)/shard_map/ppermute | solution.py:15
  35.0 9.6 %collective-permute-start.6 = (f32[64,10,1]{2,0,1:T(8,128)S(1)}, f32[64,10,1]{2,0,1:T(8,128)S(1)}, u32[]{:S(2)}, u32[]{:S(2)}) collective-permute-start(f32[64,10,1]{2,0,1:T(8,128)S(1)} %get-tuple-element.11), channel_id=1, source_target_pairs={{0,1},{1,2},{2,3},{3,4},{4,5},{5,6},{6,7},{7,8},{8,9},{9,10},{10,1... | collective-permute-start | bytes 7688 | tf_op jit(solution)/shard_map/ppermute | solution.py:12
  36.9 9.4 %collective-permute-start.7 = (f32[64,10,1]{2,0,1:T(8,128)S(1)}, f32[64,10,1]{2,0,1:T(8,128)S(1)}, u32[]{:S(2)}, u32[]{:S(2)}) collective-permute-start(f32[64,10,1]{2,0,1:T(8,128)S(1)} %get-tuple-element.12), channel_id=1, source_target_pairs={{1,0},{2,1},{3,2},{4,3},{5,4},{6,5},{7,6},{8,7},{9,8},{10,9},{11,1... | collective-permute-start | bytes 7688 | tf_op jit(solution)/shard_map/ppermute | solution.py:15
  48.1 0.7 copy-start.4
